TPU v7x, 32 devices: a whole 2x2x4 slice. The times are simulated.
32 devices in a mesh: gz: 8 (over z, x), gy: 4 (over y, core).
Axes of the slice: x: 2, y: 2, z: 4, core: 2. Of those that a mesh axis runs over, the one named last changes fastest.
Arguments:
- fields: float32 [2, 256, 256, 128], P(None, 'gz', 'gy'), may hold values from -7 to 8
- residual: float32 [2, 256, 256, 128], P(None, 'gz', 'gy'), may hold values from -14 to 14
- past_fields: float32 [20, 2, 256, 256, 128], P(None, None, 'gz', 'gy'), may hold values from -7 to 8
- past_residuals: float32 [20, 2, 256, 256, 128], P(None, None, 'gz', 'gy'), may hold values from -14 to 14
Outputs:
- new_fields: float32 [2, 256, 256, 128], P(None, 'gz', 'gy')
- summary: float32 [3], replicated
All inputs are finite; a program needn't handle non-finite values.
Results may differ from a plain program's by a relative error of at most 0.0003.
Values sent between devices are 32-bit elements; how exact they have to be, the bound alone decides.
A program may use at most 192 MiB of HBM per device.

v0:
```python
import math
import jax
import jax.numpy as jnp
from jax import lax
from jax.sharding import PartitionSpec as P

CHI_N = 20.0
RIDGE = 0.01
STEP_LOCAL = 0.1
EXACT = lax.Precision.HIGHEST


def kernel_total(length):
    decay_len = length / 4.0
    offsets = lax.iota(jnp.int32, length).astype(jnp.float32)
    return jnp.sum(jnp.cosh((0.5 * length - offsets) / decay_len))


def kernel_rows(row_first, row_count, col_first, col_count, length):
    decay_len = length / 4.0
    row_index = row_first + lax.iota(jnp.int32, row_count)[:, None]
    col_index = col_first + lax.iota(jnp.int32, col_count)[None, :]
    lag = jnp.mod(row_index - col_index, length).astype(jnp.float32)
    return jnp.cosh((0.5 * length - lag) / decay_len) / kernel_total(length)


def end_moments(first, count, length):
    decay_len = length / 4.0
    place = (first + lax.iota(jnp.int32, count)).astype(jnp.float32) / decay_len
    return jnp.stack([jnp.exp(place), jnp.exp(-place)])


def far_weights(first, count, own_block, blocks, length):
    decay_len = length / 4.0
    place = (first + lax.iota(jnp.int32, count)).astype(jnp.float32) / decay_len
    block_index = lax.iota(jnp.int32, blocks)
    below = block_index < own_block
    above = block_index > own_block
    wide = math.exp(0.5 * length / decay_len)
    rising = jnp.where(below, wide, jnp.where(above, 1.0 / wide, 0.0))
    falling = jnp.where(below, 1.0 / wide, jnp.where(above, wide, 0.0))
    factor = 0.5 / kernel_total(length)
    weight_rising = factor * jnp.exp(-place)[:, None] * rising[None, :]
    weight_falling = factor * jnp.exp(place)[:, None] * falling[None, :]
    return jnp.stack([weight_rising, weight_falling], axis=2).reshape(count, 2 * blocks)


def shards(fields, residual, past_fields, past_residuals):
    history = past_residuals.shape[0]
    species, height_cells, width_cells, line_cells = residual.shape
    height_total = height_cells * lax.axis_size("gz")
    width_total = width_cells * lax.axis_size("gy")
    cell_total = height_total * width_total * line_cells
    flat_residual = residual.reshape(-1)
    past_rows = past_residuals.reshape(history, -1)
    deltas = flat_residual[None, :] - past_rows
    gram_local = jnp.dot(deltas, deltas.T, precision=EXACT, preferred_element_type=jnp.float32)
    intersect_local = jnp.dot(
        deltas, flat_residual, precision=EXACT, preferred_element_type=jnp.float32
    )
    residual_square = jnp.sum(residual * residual)
    field_square = jnp.sum(fields * fields)
    gram_matrix, intersect = lax.psum((gram_local, intersect_local), ("gz", "gy"))
    diagonal_shift = RIDGE * jnp.trace(gram_matrix) / history + 1.0
    system = gram_matrix + diagonal_shift * jnp.eye(history, dtype=jnp.float32)
    factor = jnp.linalg.cholesky(system)
    forward = lax.linalg.triangular_solve(factor, intersect[:, None], left_side=True, lower=True)
    coeffs = lax.linalg.triangular_solve(
        factor, forward, left_side=True, lower=True, transpose_a=True
    )[:, 0]
    remain_weight = 1.0 - jnp.sum(coeffs)
    field_mixed = remain_weight * fields + jnp.dot(
        coeffs,
        past_fields.reshape(history, -1),
        precision=EXACT,
        preferred_element_type=jnp.float32,
    ).reshape(fields.shape)
    residual_mixed = remain_weight * residual + jnp.dot(
        coeffs, past_rows, precision=EXACT, preferred_element_type=jnp.float32
    ).reshape(residual.shape)
    height_first = lax.axis_index("gz") * height_cells
    width_first = lax.axis_index("gy") * width_cells
    moments = jnp.einsum(
        "ab,sbyx->sayx",
        end_moments(height_first, height_cells, height_total),
        residual_mixed,
        precision=EXACT,
    )
    every_end = lax.all_gather(moments, "gz", axis=1, tiled=True)
    near = jnp.einsum(
        "ab,sbyx->sayx",
        kernel_rows(height_first, height_cells, height_first, height_cells, height_total),
        residual_mixed,
        precision=EXACT,
    )
    far = jnp.einsum(
        "ab,sbyx->sayx",
        far_weights(
            height_first, height_cells, lax.axis_index("gz"), lax.axis_size("gz"), height_total
        ),
        every_end,
        precision=EXACT,
    )
    smoothed_half = near + far
    portion = lax.all_gather(smoothed_half, "gy", axis=2, tiled=True)
    kernel = kernel_rows(width_first, width_cells, jnp.int32(0), portion.shape[2], width_total)
    smoothed = jnp.zeros_like(smoothed_half) + jnp.einsum(
        "ab,szbx->szax", kernel, portion, precision=EXACT
    )
    new_fields = field_mixed + STEP_LOCAL * residual_mixed + smoothed
    split_field = new_fields[0] - new_fields[1]
    sum_field = new_fields[0] + new_fields[1]
    energy_local = jnp.sum(split_field * split_field / (4.0 * CHI_N) - 0.5 * sum_field)
    peak_local = jnp.max(jnp.abs(residual_mixed))
    energy_total, residual_total, field_total = lax.psum(
        (energy_local, residual_square, field_square), ("gz", "gy")
    )
    largest = lax.pmax(peak_local, ("gz", "gy"))
    relative = jnp.sqrt(residual_total / (field_total + 1.0))
    summary = jnp.stack([energy_total / cell_total, relative, largest])
    return (new_fields, summary)


def solution(mesh):
    placed = (
        P(None, "gz", "gy", None),
        P(None, "gz", "gy", None),
        P(None, None, "gz", "gy", None),
        P(None, None, "gz", "gy", None),
    )
    return jax.shard_map(
        shards,
        mesh=mesh,
        in_specs=placed,
        out_specs=(P(None, "gz", "gy", None), P()),
        check_vma=False,
    )
```

profile of v0, /device:TPU:0, one launch (start us, length us, event | category | flops | bytes accessed | tf_op | source)
XLA Modules:
  0.0 577.8 jit_solution(16843497883057855397)
XLA Ops:
  7.2 32.5 %broadcast_subtract_fusion = f32[20,2,32,64,128]{4,3,2,1,0:T(8,128)} fusion(f32[20,2,32,64,128]{4,3,2,1,0:T(8,128)} %param.7, f32[2,32,64,128]{3,2,1,0:T(8,128)} %param.5), kind=kLoop, calls=%fused_computation.8 | loop fusion | flops 10485760 | bytes 85983232 | tf_op jit(solution)/shard_map/sub | solution.py:56
  39.8 110.5 %fusion.21 = f32[20,20]{1,0:T(8,128)S(1)} fusion(f32[20,2,32,64,128]{4,3,2,1,0:T(8,128)} %broadcast_subtract_fusion), kind=kOutput, calls=%fused_computation.22 | convolution fusion | flops 2516582400 | bytes 41944640 | tf_op jit(solution)/shard_map/dot_general | solution.py:57
  150.2 75.0 %fusion.24 = f32[20]{0:T(128)S(1)} fusion(f32[2,32,64,128,1]{3,4,2,1,0:T(1,128)S(1)} %bitcast.108, f32[20,2,32,64,128]{4,3,2,1,0:T(8,128)} %broadcast_subtract_fusion), kind=kOutput, calls=%fused_computation.24 | convolution fusion | flops 125829120 | bytes 44040272 | tf_op jit(solution)/shard_map/dot_general | solution.py:58
  225.2 42.1 %all-reduce.1 = (f32[20,20]{1,0:T(8,128)S(1)}, f32[20]{0:T(128)S(1)}) all-reduce(f32[20,20]{1,0:T(8,128)S(1)} %fusion.21, f32[20]{0:T(128)S(1)} %fusion.24), channel_id=1, replica_groups=mesh['gz'=8,'gy'=4] {'gz','gy'}, use_global_device_ids=true, to_apply=%region_0.0 | all-reduce | flops 420 | bytes 3360 | tf_op jit(solution)/shard_map/psum | solution.py:63
  268.7 1.8 cholesky.17
  271.2 0.6 fusion.69
  271.9 1.5 custom-call.8
  273.6 0.8 bitcast_reduce_fusion
  275.0 74.0 %fusion.4 = f32[1,2,32,64,128]{4,0,3,2,1:T(1,128)S(1)} fusion(f32[2,32,64,128,20]{3,2,1,0,4:T(8,128)} %bitcast.106, f32[1,20]{1,0:T(1,128)S(1)} %get-tuple-element.11), kind=kOutput, calls=%fused_computation.4 | convolution fusion | flops 125829120 | bytes 44040272 | tf_op jit(solution)/shard_map/dot_general | solution.py:78
  349.0 1.3 abs_reduce_fusion
  350.3 2.4 fusion.18
  352.7 0.7 copy.17
  353.4 0.7 add_reduce_fusion
  355.0 38.6 %all-gather.3.cloned.1.call-done = f32[2,16,64,128]{3,2,0,1:T(8,128)} async-done(((f32[2,2,64,128]{3,2,0,1:T(8,128)}), f32[2,16,64,128]{3,2,0,1:T(8,128)}) %all-gather.3.cloned.1.call-update) | async-done | bytes 1048592 | tf_op jit(solution)/shard_map/all_gather | solution.py:89
  393.6 3.5 fusion.27
  397.1 5.3 add_bitcast_fusion
  402.5 39.2 %pmax.7 = f32[1]{0:T(128)} all-reduce(f32[1]{0:T(128)} %bitcast.37), channel_id=1, replica_groups=mesh['gz'=8,'gy'=4] {'gz','gy'}, use_global_device_ids=true, to_apply=%region_14.15 | all-reduce | flops 1 | bytes 8 | tf_op jit(solution)/shard_map/pmax | solution.py:118
  441.7 2.7 multiply_reduce_fusion
  444.4 63.8 %fusion.6 = f32[1,2,32,64,128]{4,0,3,2,1:T(1,128)} fusion(f32[2,32,64,128,20]{3,2,1,0,4:T(8,128)} %bitcast.107, f32[1,20]{1,0:T(1,128)S(1)} %get-tuple-element.11), kind=kOutput, calls=%fused_computation.6 | convolution fusion | flops 125829120 | bytes 44040272 | tf_op jit(solution)/shard_map/dot_general | solution.py:72
  508.2 15.2 %bitcast_add_fusion = f32[2,32,64,128]{3,2,1,0:T(8,128)S(1)} fusion(f32[2,32,64,128]{3,2,1,0:T(8,128)S(1)} %get-tuple-element.8, f32[2,32,64,128]{3,2,1,0:T(8,128)} %bitcast.109, f32[2,32,64,128]{3,2,1,0:T(8,128)} %param.4, f32[2,32,256,128]{3,1,2,0:T(8,128)} %all-gather.5.cloned.1.call-done, f32[]{:T(128)S(6)} %sub.67, f32[]{:T(128)} %add_reduce_fusion, ...), kind=kOutput, calls=%fused_computation.11 | convolution fusion | flops 1613545472 | bytes 16777480 | tf_op jit(solution)/shard_map/ab,szbx->szax/dot_general | solution.py:107
  523.5 1.3 copy-done.2
  524.8 0.9 subtract_reduce_fusion
  525.7 41.7 %all-reduce = (f32[]{:T(128)}, f32[]{:T(128)}, f32[]{:T(128)}) all-reduce(f32[]{:T(128)} %get-tuple-element.9, f32[]{:T(128)} %multiply_reduce_fusion, f32[]{:T(128)} %subtract_reduce_fusion), channel_id=1, replica_groups=mesh['gz'=8,'gy'=4] {'gz','gy'}, use_global_device_ids=true, to_apply=%region_10.11 | all-reduce | flops 3 | bytes 24 | tf_op jit(solution)/shard_map/psum | solution.py:115
  569.4 1.1 pad_maximum_fusion.1
  (25 shorter events, 1.9 us)
Async XLA Ops:
  7.2 386.5 %all-gather.3.cloned.1.call-start = ((), (), s32[]{:S(2)}) async-start(), calls=%async_computation | async-start | bytes 1179648 | tf_op jit(solution)/shard_map/all_gather | solution.py:89
  39.7 110.5 %copy-start = (f32[2,32,64,128]{3,2,1,0:T(8,128)S(1)}, f32[2,32,64,128]{3,2,1,0:T(8,128)}, u32[]{:S(2)}) copy-start(f32[2,32,64,128]{3,2,1,0:T(8,128)} %param.5) | copy-start | bytes 6291460
  275.0 74.0 %copy-start.1 = (f32[2,32,64,128]{3,2,1,0:T(8,128)S(1)}, f32[2,32,64,128]{3,2,1,0:T(8,128)}, u32[]{:S(2)}) copy-start(f32[2,32,64,128]{3,2,1,0:T(8,128)} %param.5) | copy-start | bytes 6291460
  353.4 154.9 %all-gather.5.cloned.1.call-start = ((), (), s32[]{:S(2)}) async-start(), calls=%async_computation.1 | async-start | bytes 10485760 | tf_op jit(solution)/shard_map/all_gather | solution.py:105
  523.4 1.3 copy-start.2
Sparse Core Ops, SparseCore 0:
  353.5 40.0 all-gather.2
  402.6 57.8 all-gather.4
where the time goes:
time: 588 us; the launch traced here: 578 us
  matrix products  351 us (60%)
  blocking collectives  123 us (21%)
  other arithmetic  44.7 us (8%)
  waiting for transfers between devices  38.7 us (7%)
  between operations  18.6 us (3%)
    dot_general x1, matrix products, shards(): jnp.dot(deltas, deltas.T, precision=EXACT, preferred_element_type=jnp.flo...  110 us
    dot_general x1, matrix products, shards(): jnp.dot(deltas, flat_residual, precision=EXACT, preferred_element_type=jn...  75 us
    dot_general x1, matrix products, shards(): jnp.dot(coeffs, past_rows, precision=EXACT, preferred_element_type=jnp.fl...  74 us
    dot_general x1, matrix products, shards(): jnp.dot(coeffs, past_fields.reshape(history, -1), precision=EXACT, prefer...  63.8 us
    psum x1, blocking collectives, shards(): lax.psum((gram_local, intersect_local), ('gz', 'gy'))  42.1 us
    psum x1, blocking collectives, shards(): lax.psum((energy_local, residual_square, field_square), ('gz', 'gy'))  41.7 us
    pmax x1, blocking collectives, shards(): largest = lax.pmax(peak_local, ('gz', 'gy'))  39.2 us
    all_gather x1, waiting for transfers between devices, shards(): every_end = lax.all_gather(moments, 'gz', axis=1, tiled=True)  38.6 us
  transfers between devices with their start and end apart: 2, of which 1 were waited for; matrix products, arithmetic and copies ran while one was open for 12% of the time, Pallas kernels for 0%

commit v1 on v0

--- a/solution.py
+++ b/solution.py
@@ -112,8 +112,8 @@
     sum_field = new_fields[0] + new_fields[1]
     energy_local = jnp.sum(split_field * split_field / (4.0 * CHI_N) - 0.5 * sum_field)
     peak_local = jnp.max(jnp.abs(residual_mixed))
-    energy_total, residual_total, field_total = lax.psum(
-        (energy_local, residual_square, field_square), ("gz", "gy")
+    energy_total, residual_total, field_total = jax.lax.psum(
+        jax.lax.psum((energy_local, residual_square, field_square), "gy"), "gz"
     )
     largest = lax.pmax(peak_local, ("gz", "gy"))
     relative = jnp.sqrt(residual_total / (field_total + 1.0))

time: 588 us -> 574 us (0.976)
  blocking collectives: 123 us -> 109 us
    psum x1 -> x2, blocking collectives: 41.7 us -> 27.6 us  [the longest x1 20.1 us: shards(): jax.lax.psum(jax.lax.psum((energy_local, residual_square, field_square),...]
where the time goes in v1:
time: 574 us; the launch traced here: 564 us
  matrix products  351 us (61%)
  blocking collectives  109 us (19%)
  other arithmetic  44.8 us (8%)
  waiting for transfers between devices  38.7 us (7%)
  between operations  18.5 us (3%)
    dot_general x1, matrix products, shards(): jnp.dot(deltas, deltas.T, precision=EXACT, preferred_element_type=jnp.flo...  110 us
    dot_general x1, matrix products, shards(): jnp.dot(deltas, flat_residual, precision=EXACT, preferred_element_type=jn...  75 us
    dot_general x1, matrix products, shards(): jnp.dot(coeffs, past_rows, precision=EXACT, preferred_element_type=jnp.fl...  74 us
    dot_general x1, matrix products, shards(): jnp.dot(coeffs, past_fields.reshape(history, -1), precision=EXACT, prefer...  63.8 us
    psum x1, blocking collectives, shards(): lax.psum((gram_local, intersect_local), ('gz', 'gy'))  42.1 us
    pmax x1, blocking collectives, shards(): largest = lax.pmax(peak_local, ('gz', 'gy'))  39.2 us
    all_gather x1, waiting for transfers between devices, shards(): every_end = lax.all_gather(moments, 'gz', axis=1, tiled=True)  38.6 us
    sub x1, other arithmetic, shards(): deltas = flat_residual[None, :] - past_rows  32.5 us
  transfers between devices with their start and end apart: 2, of which 1 were waited for; matrix products, arithmetic and copies ran while one was open for 12% of the time, Pallas kernels for 0%

profile of v1, /device:TPU:0, one launch (start us, length us, event | category | flops | bytes accessed | tf_op | source)
XLA Modules:
  0.0 563.6 jit_solution(5206733930420624960)
XLA Ops:
  7.2 32.5 %broadcast_subtract_fusion = f32[20,2,32,64,128]{4,3,2,1,0:T(8,128)} fusion(f32[20,2,32,64,128]{4,3,2,1,0:T(8,128)} %param.7, f32[2,32,64,128]{3,2,1,0:T(8,128)} %param.5), kind=kLoop, calls=%fused_computation.8 | loop fusion | flops 10485760 | bytes 85983232 | tf_op jit(solution)/shard_map/sub | solution.py:56
  39.8 110.5 %fusion.21 = f32[20,20]{1,0:T(8,128)S(1)} fusion(f32[20,2,32,64,128]{4,3,2,1,0:T(8,128)} %broadcast_subtract_fusion), kind=kOutput, calls=%fused_computation.22 | convolution fusion | flops 2516582400 | bytes 41944640 | tf_op jit(solution)/shard_map/dot_general | solution.py:57
  150.2 75.0 %fusion.24 = f32[20]{0:T(128)S(1)} fusion(f32[2,32,64,128,1]{3,4,2,1,0:T(1,128)S(1)} %bitcast.108, f32[20,2,32,64,128]{4,3,2,1,0:T(8,128)} %broadcast_subtract_fusion), kind=kOutput, calls=%fused_computation.24 | convolution fusion | flops 125829120 | bytes 44040272 | tf_op jit(solution)/shard_map/dot_general | solution.py:58
  225.2 42.1 %all-reduce = (f32[20,20]{1,0:T(8,128)S(1)}, f32[20]{0:T(128)S(1)}) all-reduce(f32[20,20]{1,0:T(8,128)S(1)} %fusion.21, f32[20]{0:T(128)S(1)} %fusion.24), channel_id=1, replica_groups=mesh['gz'=8,'gy'=4] {'gz','gy'}, use_global_device_ids=true, to_apply=%region_0.0 | all-reduce | flops 420 | bytes 3360 | tf_op jit(solution)/shard_map/psum | solution.py:63
  268.8 1.8 cholesky.17
  271.9 1.5 custom-call.8
  273.6 0.8 bitcast_reduce_fusion
  275.0 74.0 %fusion.4 = f32[1,2,32,64,128]{4,0,3,2,1:T(1,128)S(1)} fusion(f32[2,32,64,128,20]{3,2,1,0,4:T(8,128)} %bitcast.106, f32[1,20]{1,0:T(1,128)S(1)} %get-tuple-element.14), kind=kOutput, calls=%fused_computation.4 | convolution fusion | flops 125829120 | bytes 44040272 | tf_op jit(solution)/shard_map/dot_general | solution.py:78
  349.0 1.2 abs_reduce_fusion
  350.2 2.4 fusion.18
  352.6 0.7 copy.17
  353.3 0.7 add_reduce_fusion
  354.9 38.6 %all-gather.3.cloned.1.call-done = f32[2,16,64,128]{3,2,0,1:T(8,128)} async-done(((f32[2,2,64,128]{3,2,0,1:T(8,128)}), f32[2,16,64,128]{3,2,0,1:T(8,128)}) %all-gather.3.cloned.1.call-update) | async-done | bytes 1048592 | tf_op jit(solution)/shard_map/all_gather | solution.py:89
  393.5 3.5 fusion.27
  397.0 5.3 add_bitcast_fusion
  402.4 39.2 %pmax.7 = f32[1]{0:T(128)} all-reduce(f32[1]{0:T(128)} %bitcast.37), channel_id=1, replica_groups=mesh['gz'=8,'gy'=4] {'gz','gy'}, use_global_device_ids=true, to_apply=%region_17.18 | all-reduce | flops 1 | bytes 8 | tf_op jit(solution)/shard_map/pmax | solution.py:118
  441.6 2.7 multiply_reduce_fusion
  444.3 63.8 %fusion.6 = f32[1,2,32,64,128]{4,0,3,2,1:T(1,128)} fusion(f32[2,32,64,128,20]{3,2,1,0,4:T(8,128)} %bitcast.107, f32[1,20]{1,0:T(1,128)S(1)} %get-tuple-element.14), kind=kOutput, calls=%fused_computation.6 | convolution fusion | flops 125829120 | bytes 44040272 | tf_op jit(solution)/shard_map/dot_general | solution.py:72
  508.2 15.2 %bitcast_add_fusion = f32[2,32,64,128]{3,2,1,0:T(8,128)S(1)} fusion(f32[2,32,64,128]{3,2,1,0:T(8,128)S(1)} %get-tuple-element.11, f32[2,32,64,128]{3,2,1,0:T(8,128)} %bitcast.109, f32[2,32,64,128]{3,2,1,0:T(8,128)} %param.4, f32[2,32,256,128]{3,1,2,0:T(8,128)} %all-gather.5.cloned.1.call-done, f32[]{:T(128)S(6)} %sub.67, f32[]{:T(128)} %add_reduce_fusion, ...), kind=kOutput, calls=%fused_computation.11 | convolution fusion | flops 1613545472 | bytes 16777480 | tf_op jit(solution)/shard_map/ab,szbx->szax/dot_general | solution.py:107
  523.4 1.3 copy-done.2
  524.7 0.9 subtract_reduce_fusion
  525.6 7.5 %all-reduce.2 = (f32[]{:T(128)}, f32[]{:T(128)}, f32[]{:T(128)}) all-reduce(f32[]{:T(128)} %get-tuple-element.12, f32[]{:T(128)} %multiply_reduce_fusion, f32[]{:T(128)} %subtract_reduce_fusion), channel_id=1, replica_groups=mesh['gz'=8,'gy'=4] {'gy'}, use_global_device_ids=true, to_apply=%region_11.12 | all-reduce | flops 3 | bytes 24 | tf_op jit(solution)/shard_map/psum | solution.py:116
  533.1 20.1 %all-reduce.1 = (f32[]{:T(128)}, f32[]{:T(128)}, f32[]{:T(128)}) all-reduce(f32[]{:T(128)} %get-tuple-element.7, f32[]{:T(128)} %get-tuple-element.8, f32[]{:T(128)} %get-tuple-element.9), channel_id=1, replica_groups=mesh['gz'=8,'gy'=4] {'gz'}, use_global_device_ids=true, to_apply=%region_12.13 | all-reduce | flops 3 | bytes 24 | tf_op jit(solution)/shard_map/psum | solution.py:115
  555.1 1.3 pad_maximum_fusion.1
  (26 shorter events, 2.5 us)
Async XLA Ops:
  7.2 386.4 %all-gather.3.cloned.1.call-start = ((), (), s32[]{:S(2)}) async-start(), calls=%async_computation | async-start | bytes 1179648 | tf_op jit(solution)/shard_map/all_gather | solution.py:89
  39.7 110.5 %copy-start = (f32[2,32,64,128]{3,2,1,0:T(8,128)S(1)}, f32[2,32,64,128]{3,2,1,0:T(8,128)}, u32[]{:S(2)}) copy-start(f32[2,32,64,128]{3,2,1,0:T(8,128)} %param.5) | copy-start | bytes 6291460
  275.0 74.0 %copy-start.1 = (f32[2,32,64,128]{3,2,1,0:T(8,128)S(1)}, f32[2,32,64,128]{3,2,1,0:T(8,128)}, u32[]{:S(2)}) copy-start(f32[2,32,64,128]{3,2,1,0:T(8,128)} %param.5) | copy-start | bytes 6291460
  353.3 154.9 %all-gather.5.cloned.1.call-start = ((), (), s32[]{:S(2)}) async-start(), calls=%async_computation.1 | async-start | bytes 10485760 | tf_op jit(solution)/shard_map/all_gather | solution.py:105
  523.4 1.3 copy-start.2
Sparse Core Ops, SparseCore 0:
  353.4 40.0 all-gather.2
  402.5 57.8 all-gather.4
